TPU v7x, 512 devices: a whole 4x4x16 slice. The times are simulated.
512 devices in a mesh: gy: 32 (over z, core), gx: 16 (over x, y).
Axes of the slice: x: 4, y: 4, z: 16, core: 2. Of those that a mesh axis runs over, the one named last changes fastest.
Arguments:
- level_in: bfloat16 [256, 1024, 128], P('gy', 'gx'), may hold values from -6 to 6
- w_level: bfloat16 [3, 3, 128, 128], replicated, may hold values from -0.1875 to 0.1875
- w_down: bfloat16 [2, 2, 128, 256], replicated, may hold values from -0.25 to 0.25
- w_neck: bfloat16 [3, 3, 256, 256], replicated, may hold values from -0.125 to 0.125
- cotangent: bfloat16 [128, 512, 256], P('gy', None, 'gx'), may hold values from -6 to 6
Outputs:
- neck_out: bfloat16 [128, 512, 256], P('gy', None, 'gx')
- grad_input: bfloat16 [256, 1024, 128], P('gy', 'gx')
- grad_level: bfloat16 [3, 3, 128, 128], replicated
- grad_down: bfloat16 [2, 2, 128, 256], replicated
- grad_neck: bfloat16 [3, 3, 256, 256], replicated
All inputs are finite; a program needn't handle non-finite values.
Results may differ from a plain program's by a relative error of at most 0.012.
Values may be sent and summed in bfloat16 or wider, within the bound.
A program may use at most 64 MiB of HBM per device.

v0:
```python
import math
import jax
import jax.numpy as jnp
from jax import lax
from jax.sharding import PartitionSpec as P


def extended(cells, sides, width):
    for axis, dim in sides:
        count = lax.axis_size(axis)
        ends = count - 1
        head = lax.slice_in_dim(cells, 0, width, axis=dim)
        tail = lax.slice_in_dim(cells, cells.shape[dim] - width, cells.shape[dim], axis=dim)
        cells = jnp.concatenate(
            [
                lax.ppermute(tail, axis, [(i, (i + 1) % count) for i in range(ends)]),
                cells,
                lax.ppermute(head, axis, [((i + 1) % count, i) for i in range(ends)]),
            ],
            axis=dim,
        )
    return cells


def slope_of(value):
    gate = jax.nn.sigmoid(value)
    return gate + value * gate * (1.0 - gate)


def tile_rims(field_in):
    return extended(field_in, (("gy", 0), ("gx", 1)), 1)


def conv_padded(padded, weights):
    row_count = padded.shape[0] - 2
    col_count = padded.shape[1] - 2
    result = jnp.zeros((row_count * col_count, weights.shape[3]), jnp.float32)
    for offset_y in range(3):
        for offset_x in range(3):
            window = padded[offset_y : offset_y + row_count, offset_x : offset_x + col_count]
            window = window.reshape(row_count * col_count, padded.shape[2])
            result = result + jnp.dot(
                window, weights[offset_y, offset_x], preferred_element_type=jnp.float32
            )
    return result


def weight_terms(padded, grads):
    row_count = grads.shape[0]
    col_count = grads.shape[1]
    flat_grads = grads.reshape(row_count * col_count, grads.shape[2])
    kernel_rows = []
    for offset_y in range(3):
        kernel_row = []
        for offset_x in range(3):
            window = padded[offset_y : offset_y + row_count, offset_x : offset_x + col_count]
            window = window.reshape(row_count * col_count, padded.shape[2])
            kernel_row.append(
                lax.dot_general(
                    window, flat_grads, (((0,), (0,)), ((), ())), preferred_element_type=jnp.float32
                )
            )
        kernel_rows.append(jnp.stack(kernel_row))
    return jnp.stack(kernel_rows)


def local(level_in, w_level, w_down, w_neck, cotangent):
    tile_rows = level_in.shape[0]
    tile_cols = level_in.shape[1]
    level_width = level_in.shape[2]
    neck_width = w_neck.shape[3]
    half_rows = tile_rows // 2
    half_cols = tile_cols // 2
    level_pad = tile_rims(level_in)
    level_pre = conv_padded(level_pad, w_level)
    level_flat = level_in.reshape(tile_rows * tile_cols, level_width).astype(jnp.float32)
    level_act = (level_flat + jax.nn.silu(level_pre)).astype(jnp.bfloat16)
    level_grid = level_act.reshape(half_rows, 2, half_cols, 2, level_width)
    neck_in = jnp.einsum(
        "hpwqc,pqcd->hwd", level_grid, w_down, preferred_element_type=jnp.float32
    ).astype(jnp.bfloat16)
    neck_pad = tile_rims(neck_in)
    neck_pre = conv_padded(neck_pad, w_neck)
    neck_flat = neck_in.reshape(half_rows * half_cols, neck_width).astype(jnp.float32)
    neck_tile = (
        (neck_flat + jax.nn.silu(neck_pre))
        .astype(jnp.bfloat16)
        .reshape(half_rows, half_cols, neck_width)
    )
    neck_out = lax.all_to_all(neck_tile, "gx", split_axis=2, concat_axis=1, tiled=True)
    neck_cot = lax.all_to_all(cotangent, "gx", split_axis=1, concat_axis=2, tiled=True)
    cot_flat = neck_cot.reshape(half_rows * half_cols, neck_width).astype(jnp.float32)
    neck_gate = (
        (cot_flat * slope_of(neck_pre))
        .astype(jnp.bfloat16)
        .reshape(half_rows, half_cols, neck_width)
    )
    flip_neck = jnp.transpose(w_neck[::-1, ::-1], (0, 1, 3, 2))
    gate_pad = tile_rims(neck_gate)
    neck_back = conv_padded(gate_pad, flip_neck)
    cot_tile = neck_cot.reshape(half_rows * half_cols, neck_width).astype(jnp.float32)
    neck_grad = (
        (cot_tile + neck_back).astype(jnp.bfloat16).reshape(half_rows, half_cols, neck_width)
    )
    neck_wgrad = weight_terms(neck_pad, neck_gate)
    level_back = jnp.einsum(
        "hwd,pqcd->hpwqc", neck_grad, w_down, preferred_element_type=jnp.float32
    )
    level_back = level_back.reshape(tile_rows * tile_cols, level_width)
    down_wgrad = jnp.einsum(
        "hpwqc,hwd->pqcd", level_grid, neck_grad, preferred_element_type=jnp.float32
    )
    level_gate = (
        (level_back * slope_of(level_pre))
        .astype(jnp.bfloat16)
        .reshape(tile_rows, tile_cols, level_width)
    )
    flip_level = jnp.transpose(w_level[::-1, ::-1], (0, 1, 3, 2))
    level_gpad = tile_rims(level_gate)
    grad_input = (level_back + conv_padded(level_gpad, flip_level)).astype(jnp.bfloat16)
    grad_input = grad_input.reshape(tile_rows, tile_cols, level_width)
    level_wgrad = weight_terms(level_pad, level_gate)
    device_count = lax.axis_size("gy") * lax.axis_size("gx")
    level_count = tile_rows * tile_cols * device_count
    level_scale = 1.0 / math.sqrt(level_count)
    neck_scale = 1.0 / math.sqrt(level_count // 4)
    reduced = lax.psum((level_wgrad, down_wgrad, neck_wgrad), ("gy", "gx"))
    grad_level = (reduced[0] * level_scale).astype(jnp.bfloat16)
    grad_down = (reduced[1] * neck_scale).astype(jnp.bfloat16)
    grad_neck = (reduced[2] * neck_scale).astype(jnp.bfloat16)
    return (neck_out, grad_input, grad_level, grad_down, grad_neck)


def solution(mesh):
    return jax.shard_map(
        local,
        mesh=mesh,
        in_specs=(P("gy", "gx", None), P(), P(), P(), P("gy", None, "gx")),
        out_specs=(P("gy", None, "gx"), P("gy", "gx", None), P(), P(), P()),
        check_vma=False,
    )
```

profile of v0, /device:TPU:2, one launch (start us, length us, event | category | flops | bytes accessed | tf_op | source)
XLA Modules:
  0.0 618.8 jit_solution(6595421685957169687)
XLA Ops:
  7.2 1.3 copy.37
  8.5 1.2 reshape.213
  9.7 9.2 %all-to-all-start.1 = ((bf16[16,2,1024]{2,1,0:T(2,128)(2,1)}), bf16[16,2,1024]{2,1,0:T(2,128)(2,1)S(1)}, u32[]{:S(2)}, u32[]{:S(2)}) async-start(bf16[16,2,1024]{2,1,0:T(2,128)(2,1)} %reshape.213), calls=%async_computation.1 | async-start | bytes 131072 | tf_op jit(solution)/shard_map/all_to_all | solution.py:91
  18.9 1.3 collective-permute-start
  20.2 1.4 collective-permute-start.1
  21.8 2.1 collective-permute-done.1
  24.0 3.4 collective-permute-start.2
  27.4 4.6 collective-permute-start.3
  32.3 1.0 collective-permute-done.3
  34.7 0.9 add_convert_fusion
  36.5 1.3 collective-permute-start.5
  37.8 3.9 collective-permute-start.4
  42.5 2.7 collective-permute-start.6
  45.2 5.3 collective-permute-start.7
  52.8 0.8 convolution_add_fusion.21
  53.6 0.8 fusion.19
  54.5 1.2 reshape.214
  55.6 1.4 copy.38
  57.0 0.9 reshape.205
  57.9 1.0 copy.40
  59.6 1.9 multiply_convert_fusion.4
  63.2 0.9 convolution_bitcast_fusion.6
  64.1 0.9 convolution_bitcast_fusion.7
  65.0 0.9 convolution_bitcast_fusion.8
  65.9 0.9 convolution_bitcast_fusion.9
  66.9 1.0 copy.34
  67.9 0.9 reshape.211
  68.8 8.5 %all-to-all-start = ((bf16[16,2,1024]{2,1,0:T(2,128)(2,1)}), bf16[16,2,1024]{2,1,0:T(2,128)(2,1)S(1)}, u32[]{:S(2)}, u32[]{:S(2)}) async-start(bf16[16,2,1024]{2,1,0:T(2,128)(2,1)} %reshape.211), calls=%async_computation | async-start | bytes 131072 | tf_op jit(solution)/shard_map/all_to_all | solution.py:90
  77.3 1.3 collective-permute-start.9
  78.7 3.0 collective-permute-start.8
  81.9 0.9 copy-done.18
  82.9 1.5 pad_maximum_fusion
  84.5 3.4 collective-permute-start.10
  87.9 4.6 collective-permute-start.11
  92.7 1.1 collective-permute-done.11
  98.4 1.3 collective-permute-start.13
  99.7 5.1 collective-permute-start.12
  104.9 0.9 pad_maximum_fusion.1
  105.7 1.1 convolution_bitcast_fusion
  106.9 2.8 collective-permute-start.14
  109.7 5.3 collective-permute-start.15
  115.2 1.1 collective-permute-done.15
  117.9 0.9 fusion.4
  119.0 0.9 all_to_all.23
  119.9 486.5 %all-reduce.3.cloned.1.call-done = (f32[3,3,128,128]{3,2,1,0:T(8,128)}, f32[2,2,128,256]{3,2,1,0:T(8,128)}, f32[3,3,256,256]{3,2,1,0:T(8,128)}) async-done(((f32[3,3,128,128]{3,2,1,0:T(8,128)}, f32[2,2,128,256]{3,2,1,0:T(8,128)}, f32[3,3,256,256]{3,2,1,0:T(8,128)}), (f32[3,3,128,128]{3,2,1,0:T(8,128)}, f32[2,2,128,256]{3,2,1,0:T(8,128)}, f32[3,3,256,256]{3,2,1,0:T(8,128)})) %all-reduce.3.cloned.1.call-update) | async-done | bytes 3473424 | tf_op jit(solution)/shard_map/psum | solution.py:127
  606.4 1.9 multiply_convert_fusion.1
  608.3 0.7 multiply_convert_fusion.2
  609.1 2.9 multiply_convert_fusion
  (184 shorter events, 15.1 us)
Async XLA Ops:
  7.2 29.1 %copy-start = (bf16[2,2,128,256]{3,2,1,0:T(8,128)(2,1)S(1)}, bf16[2,2,128,256]{3,2,1,0:T(8,128)(2,1)}, u32[]{:S(2)}) copy-start(bf16[2,2,128,256]{3,2,1,0:T(8,128)(2,1)} %param.7) | copy-start | bytes 786436
  7.2 11.7 %copy-start.2 = (bf16[8,64,128]{2,1,0:T(8,128)(2,1)S(1)}, bf16[8,64,128]{2,1,0:T(8,128)(2,1)}, u32[]{:S(2)}) copy-start(bf16[8,64,128]{2,1,0:T(8,128)(2,1)} %param.5) | copy-start | bytes 393220
  7.2 14.5 %copy-start.1 = (bf16[3,3,256,256]{3,2,1,0:T(8,128)(2,1)S(1)}, bf16[3,3,256,256]{3,2,1,0:T(8,128)(2,1)}, u32[]{:S(2)}) copy-start(bf16[3,3,256,256]{3,2,1,0:T(8,128)(2,1)} %param.8) | copy-start | bytes 3538948
  9.7 44.8 %all-to-all-start.1 = ((bf16[16,2,1024]{2,1,0:T(2,128)(2,1)}), bf16[16,2,1024]{2,1,0:T(2,128)(2,1)S(1)}, u32[]{:S(2)}, u32[]{:S(2)}) async-start(bf16[16,2,1024]{2,1,0:T(2,128)(2,1)} %reshape.213), calls=%async_computation.1 | async-start | bytes 131072 | tf_op jit(solution)/shard_map/all_to_all | solution.py:91
  18.9 2.8 collective-permute-start
  20.2 11.7 %copy-start.16 = (bf16[3,3,128,128]{3,2,1,0:T(8,128)(2,1)S(1)}, bf16[3,3,128,128]{3,2,1,0:T(8,128)(2,1)}, u32[]{:S(2)}) copy-start(bf16[3,3,128,128]{3,2,1,0:T(8,128)(2,1)} %param.6) | copy-start | bytes 884740
  20.2 3.6 collective-permute-start.1
  23.9 9.9 %copy-start.3 = (bf16[8,64,128]{2,1,0:T(8,128)(2,1)}, bf16[8,64,128]{2,1,0:T(8,128)(2,1)S(1)}, u32[]{:S(2)}) copy-start(bf16[8,64,128]{2,1,0:T(8,128)(2,1)S(1)} %get-tuple-element.37) | copy-start | bytes 393220
  24.0 8.3 %collective-permute-start.2 = (bf16[10,1,128]{2,1,0:T(2,128)(2,1)S(1)}, bf16[10,1,128]{2,1,0:T(2,128)(2,1)S(1)}, u32[]{:S(2)}, u32[]{:S(2)}) collective-permute-start(bf16[10,1,128]{2,1,0:T(2,128)(2,1)S(1)} %get-tuple-element.27), channel_id=1, source_target_pairs={{0,1},{1,2},{2,3},{3,4},{4,5},{5,6},{6,7},{7,8},{8,9},{9,10},{10,1... | collective-permute-start | bytes 7688 | tf_op jit(solution)/shard_map/ppermute | solution.py:16
  27.4 5.9 collective-permute-start.3
  33.5 1.1 copy-start.38
  36.5 5.9 collective-permute-start.5
  37.8 4.7 collective-permute-start.4
  42.5 8.8 %collective-permute-start.6 = (bf16[6,1,256]{2,1,0:T(2,128)(2,1)S(1)}, bf16[6,1,256]{2,1,0:T(2,128)(2,1)S(1)}, u32[]{:S(2)}, u32[]{:S(2)}) collective-permute-start(bf16[6,1,256]{2,1,0:T(2,128)(2,1)S(1)} %get-tuple-element.58), channel_id=1, source_target_pairs={{0,1},{1,2},{2,3},{3,4},{4,5},{5,6},{6,7},{7,8},{8,9},{9,10},{10,1... | collective-permute-start | bytes 9224 | tf_op jit(solution)/shard_map/ppermute | solution.py:16
  45.2 6.6 %collective-permute-start.7 = (bf16[6,1,256]{2,1,0:T(2,128)(2,1)S(1)}, bf16[6,1,256]{2,1,0:T(2,128)(2,1)S(1)}, u32[]{:S(2)}, u32[]{:S(2)}) collective-permute-start(bf16[6,1,256]{2,1,0:T(2,128)(2,1)S(1)} %get-tuple-element.59), channel_id=1, source_target_pairs={{1,0},{2,1},{3,2},{4,3},{5,4},{6,5},{7,6},{8,7},{9,8},{10,9},{11,1... | collective-permute-start | bytes 9224 | tf_op jit(solution)/shard_map/ppermute | solution.py:18
  51.9 1.7 copy-start.23
  51.9 1.7 copy-start.25
  51.9 1.7 copy-start.27
  51.9 1.7 copy-start.29
  51.9 1.7 copy-start.31
  57.9 4.2 copy-start.32
  57.9 4.4 copy-start.41
  57.9 4.6 copy-start.30
  61.5 1.7 copy-start.28
  62.1 2.0 copy-start.26
  62.3 2.7 copy-start.22
  62.6 3.4 copy-start.24
  63.2 14.1 %copy-start.42 = (bf16[1,32,256]{2,1,0:T(8,128)(2,1)S(1)}, bf16[1,32,256]{2,1,0:T(8,128)(2,1)}, u32[]{:S(2)}) copy-start(bf16[1,32,256]{2,1,0:T(8,128)(2,1)} %get-tuple-element.63) | copy-start | bytes 49156
  68.8 12.9 %copy-start.17 = (f32[1,256,256]{2,1,0:T(8,128)S(1)}, f32[1,256,256]{2,1,0:T(8,128)}, u32[]{:S(2)}) copy-start(f32[1,256,256]{2,1,0:T(8,128)} %convolution_bitcast_fusion.6) | copy-start | bytes 786436
  68.8 49.9 %all-to-all-start = ((bf16[16,2,1024]{2,1,0:T(2,128)(2,1)}), bf16[16,2,1024]{2,1,0:T(2,128)(2,1)S(1)}, u32[]{:S(2)}, u32[]{:S(2)}) async-start(bf16[16,2,1024]{2,1,0:T(2,128)(2,1)} %reshape.211), calls=%async_computation | async-start | bytes 131072 | tf_op jit(solution)/shard_map/all_to_all | solution.py:90
  77.3 529.1 %all-reduce.3.cloned.1.call-start = ((), (), s32[]{:S(2)}) async-start(), calls=%async_computation.2 | async-start | bytes 6946816 | tf_op jit(solution)/shard_map/psum | solution.py:127
  77.3 7.1 %collective-permute-start.9 = (bf16[1,32,256]{2,1,0:T(8,128)(2,1)S(1)}, bf16[1,32,256]{2,1,0:T(8,128)(2,1)S(1)}, u32[]{:S(2)}, u32[]{:S(2)}) collective-permute-start(bf16[1,32,256]{2,1,0:T(8,128)(2,1)S(1)} %copy-done.42), channel_id=1, source_target_pairs={{16,0},{32,16},{48,32},{64,48},{80,64},{96,80},{112,96},{128,112},... | collective-permute-start | bytes 49160 | tf_op jit(solution)/shard_map/ppermute | solution.py:18
  78.7 5.8 collective-permute-start.8
  81.8 1.1 copy-start.20
  84.5 8.2 %collective-permute-start.10 = (bf16[6,1,256]{2,1,0:T(2,128)(2,1)S(1)}, bf16[6,1,256]{2,1,0:T(2,128)(2,1)S(1)}, u32[]{:S(2)}, u32[]{:S(2)}) collective-permute-start(bf16[6,1,256]{2,1,0:T(2,128)(2,1)S(1)} %get-tuple-element.54), channel_id=1, source_target_pairs={{0,1},{1,2},{2,3},{3,4},{4,5},{5,6},{6,7},{7,8},{8,9},{9,10},{10,1... | collective-permute-start | bytes 9224 | tf_op jit(solution)/shard_map/ppermute | solution.py:16
  87.9 5.9 collective-permute-start.11
  95.6 1.2 copy-start.39
  95.8 1.2 copy-start.14
  96.1 1.4 copy-start.12
  96.2 1.5 copy-start.10
  96.5 1.7 copy-start.8
  98.4 8.4 %collective-permute-start.13 = (bf16[1,64,128]{2,1,0:T(8,128)(2,1)S(1)}, bf16[1,64,128]{2,1,0:T(8,128)(2,1)S(1)}, u32[]{:S(2)}, u32[]{:S(2)}) collective-permute-start(bf16[1,64,128]{2,1,0:T(8,128)(2,1)S(1)} %get-tuple-element.32), channel_id=1, source_target_pairs={{16,0},{32,16},{48,32},{64,48},{80,64},{96,80},{112,96},{128,112},... | collective-permute-start | bytes 49160 | tf_op jit(solution)/shard_map/ppermute | solution.py:18
  99.7 6.0 copy-start.37
  99.7 7.1 %collective-permute-start.12 = (bf16[1,64,128]{2,1,0:T(8,128)(2,1)S(1)}, bf16[1,64,128]{2,1,0:T(8,128)(2,1)S(1)}, u32[]{:S(2)}, u32[]{:S(2)}) collective-permute-start(bf16[1,64,128]{2,1,0:T(8,128)(2,1)S(1)} %get-tuple-element.31), channel_id=1, source_target_pairs={{0,16},{16,32},{32,48},{48,64},{64,80},{80,96},{96,112},{112,128},... | collective-permute-start | bytes 49160 | tf_op jit(solution)/shard_map/ppermute | solution.py:16
  106.8 8.2 %copy-start.15 = (bf16[3,3,128,128]{2,3,1,0:T(8,128)(2,1)S(1)}, bf16[3,3,128,128]{2,3,1,0:T(8,128)(2,1)}, u32[]{:S(2)}) copy-start(bf16[3,3,128,128]{2,3,1,0:T(8,128)(2,1)} %reverse_bitcast_fusion.1) | copy-start | bytes 884740
  106.9 8.3 %collective-permute-start.14 = (bf16[10,1,128]{2,1,0:T(2,128)(2,1)S(1)}, bf16[10,1,128]{2,1,0:T(2,128)(2,1)S(1)}, u32[]{:S(2)}, u32[]{:S(2)}) collective-permute-start(bf16[10,1,128]{2,1,0:T(2,128)(2,1)S(1)} %get-tuple-element.22), channel_id=1, source_target_pairs={{0,1},{1,2},{2,3},{3,4},{4,5},{5,6},{6,7},{7,8},{8,9},{9,10},{10,1... | collective-permute-start | bytes 7688 | tf_op jit(solution)/shard_map/ppermute | solution.py:16
  109.7 6.6 %collective-permute-start.15 = (bf16[10,1,128]{2,1,0:T(2,128)(2,1)S(1)}, bf16[10,1,128]{2,1,0:T(2,128)(2,1)S(1)}, u32[]{:S(2)}, u32[]{:S(2)}) collective-permute-start(bf16[10,1,128]{2,1,0:T(2,128)(2,1)S(1)} %get-tuple-element.23), channel_id=1, source_target_pairs={{1,0},{2,1},{3,2},{4,3},{5,4},{6,5},{7,6},{8,7},{9,8},{10,9},{11,1... | collective-permute-start | bytes 7688 | tf_op jit(solution)/shard_map/ppermute | solution.py:18
  606.4 1.9 copy-start.35
  (14 other events, 11.8 us)
Sparse Core Ops, SparseCore 0:
  106.9 499.4 all-reduce.2
where the time goes:
time: 620 us; the launch traced here: 619 us
  waiting for transfers between devices  492 us (79%)
  starting transfers between devices  68.3 us (11%)
  matrix products  19 us (3%)
  between operations  15.2 us (2%)
  local copies, waits for them, and re-layouts  15 us (2%)
  other arithmetic  9.4 us (2%)
    psum x1, waiting for transfers between devices, local(): reduced = lax.psum((level_wgrad, down_wgrad, neck_wgrad), ('gy', 'gx'))  487 us
    ppermute x8, starting transfers between devices, extended(): lax.ppermute(tail, axis, [(i, (i + 1) % count) for i in range(ends)])  25.5 us
    ppermute x8, starting transfers between devices, extended(): lax.ppermute(head, axis, [((i + 1) % count, i) for i in range(ends)])  25 us
  transfers between devices with their start and end apart: 19, of which 7 were waited for; matrix products, arithmetic and copies ran while one was open for 3% of the time, Pallas kernels for 0%

commit v1 on v0

--- a/solution.py
+++ b/solution.py
@@ -124,7 +124,9 @@
     level_count = tile_rows * tile_cols * device_count
     level_scale = 1.0 / math.sqrt(level_count)
     neck_scale = 1.0 / math.sqrt(level_count // 4)
-    reduced = lax.psum((level_wgrad, down_wgrad, neck_wgrad), ("gy", "gx"))
+    reduced = (level_wgrad, down_wgrad, neck_wgrad)
+    for mesh_axis in ("gx", "gy"):
+        reduced = lax.psum(reduced, mesh_axis)
     grad_level = (reduced[0] * level_scale).astype(jnp.bfloat16)
     grad_down = (reduced[1] * neck_scale).astype(jnp.bfloat16)
     grad_neck = (reduced[2] * neck_scale).astype(jnp.bfloat16)

time: 620 us -> 460 us (0.74)
  the two profiles are of different devices: /device:TPU:2 before, /device:TPU:1 now
where the time goes in v1:
time: 460 us; the launch traced here: 459 us
  waiting for transfers between devices  348 us (76%)
  starting transfers between devices  60.5 us (13%)
  matrix products  15.6 us (3%)
  between operations  15.3 us (3%)
  local copies, waits for them, and re-layouts  10.8 us (2%)
  other arithmetic  9.43 us (2%)
    psum x2, waiting for transfers between devices, local(): reduced = lax.psum(reduced, mesh_axis)  332 us
    ppermute x8, starting transfers between devices, extended(): lax.ppermute(tail, axis, [(i, (i + 1) % count) for i in range(ends)])  32.5 us
    ppermute x8, waiting for transfers between devices, extended(): lax.ppermute(head, axis, [((i + 1) % count, i) for i in range(ends)])  14.3 us
    ppermute x8, starting transfers between devices, extended(): lax.ppermute(head, axis, [((i + 1) % count, i) for i in range(ends)])  13.1 us
    dot_general x36, matrix products, conv_padded(): jnp.dot(window, weights[offset_y, offset_x], preferred_element_type=jnp.f...  10.3 us
  transfers between devices with their start and end apart: 20, of which 8 were waited for; matrix products, arithmetic and copies ran while one was open for 3% of the time, Pallas kernels for 0%

profile of v1, /device:TPU:1, one launch (start us, length us, event | category | flops | bytes accessed | tf_op | source)
XLA Modules:
  0.0 459.3 jit_solution(10485052559811039487)
XLA Ops:
  7.2 0.8 fusion.68
  8.0 4.9 %collective-permute-start = (bf16[1,64,128]{2,1,0:T(8,128)(2,1)S(1)}, bf16[1,64,128]{2,1,0:T(8,128)(2,1)S(1)}, u32[]{:S(2)}, u32[]{:S(2)}) collective-permute-start(bf16[1,64,128]{2,1,0:T(8,128)(2,1)S(1)} %get-tuple-element.42), channel_id=1, source_target_pairs={{0,16},{16,32},{32,48},{48,64},{64,80},{80,96},{96,112},{112,128},... | collective-permute-start | bytes 49160 | tf_op jit(solution)/shard_map/ppermute | solution.py:16
  12.9 1.2 copy.37
  14.1 1.2 reshape.213
  15.3 6.8 %all-to-all-start.1 = ((bf16[16,2,1024]{2,1,0:T(2,128)(2,1)}), bf16[16,2,1024]{2,1,0:T(2,128)(2,1)S(1)}, u32[]{:S(2)}, u32[]{:S(2)}) async-start(bf16[16,2,1024]{2,1,0:T(2,128)(2,1)} %reshape.213), calls=%async_computation.1 | async-start | bytes 131072 | tf_op jit(solution)/shard_map/all_to_all | solution.py:91
  22.1 1.9 collective-permute-start.1
  24.1 3.4 collective-permute-done.1
  27.6 3.3 collective-permute-start.2
  30.9 1.3 collective-permute-start.3
  32.5 2.7 collective-permute-done.3
  36.6 0.9 add_convert_fusion
  37.8 1.9 collective-permute-start.5
  39.7 3.6 collective-permute-start.4
  43.5 0.7 collective-permute-done.4
  44.2 3.1 collective-permute-start.6
  47.3 1.3 collective-permute-start.7
  48.6 0.6 pad_maximum_fusion.13
  49.4 2.3 collective-permute-done.7
  52.7 0.8 convolution_add_fusion.21
  53.6 0.8 fusion.19
  54.4 1.2 reshape.214
  55.5 1.4 copy.38
  56.9 0.9 reshape.205
  57.9 1.0 copy.40
  58.9 1.3 multiply_convert_fusion.4
  62.3 2.1 collective-permute-start.9
  64.4 5.5 %collective-permute-start.8 = (bf16[1,32,256]{2,1,0:T(8,128)(2,1)S(1)}, bf16[1,32,256]{2,1,0:T(8,128)(2,1)S(1)}, u32[]{:S(2)}, u32[]{:S(2)}) collective-permute-start(bf16[1,32,256]{2,1,0:T(8,128)(2,1)S(1)} %get-tuple-element.65), channel_id=1, source_target_pairs={{0,16},{16,32},{32,48},{48,64},{64,80},{80,96},{96,112},{112,128},... | collective-permute-start | bytes 49160 | tf_op jit(solution)/shard_map/ppermute | solution.py:16
  70.0 1.6 pad_maximum_fusion
  71.6 4.3 collective-permute-start.10
  76.0 1.3 collective-permute-start.11
  77.5 3.1 collective-permute-done.11
  84.1 0.2 convolution_bitcast_fusion.16
  85.3 1.1 convolution_bitcast_fusion
  86.4 0.9 pad_maximum_fusion.1
  87.3 2.1 collective-permute-start.13
  89.4 4.5 collective-permute-start.12
  94.1 0.9 reshape.211
  95.0 8.1 %all-to-all-start = ((bf16[16,2,1024]{2,1,0:T(2,128)(2,1)}), bf16[16,2,1024]{2,1,0:T(2,128)(2,1)S(1)}, u32[]{:S(2)}, u32[]{:S(2)}) async-start(bf16[16,2,1024]{2,1,0:T(2,128)(2,1)} %reshape.211), calls=%async_computation | async-start | bytes 131072 | tf_op jit(solution)/shard_map/all_to_all | solution.py:90
  103.1 3.3 collective-permute-start.14
  106.4 1.3 collective-permute-start.15
  107.9 2.8 collective-permute-done.15
  111.0 115.4 %all-reduce.7.cloned.1.call-done = (f32[3,3,128,128]{3,2,1,0:T(8,128)}, f32[2,2,128,256]{3,2,1,0:T(8,128)}, f32[3,3,256,256]{3,2,1,0:T(8,128)}) async-done(((f32[3,3,128,128]{3,2,1,0:T(8,128)}, f32[2,2,128,256]{3,2,1,0:T(8,128)}, f32[3,3,256,256]{3,2,1,0:T(8,128)}), (f32[3,3,128,128]{3,2,1,0:T(8,128)}, f32[2,2,128,256]{3,2,1,0:T(8,128)}, f32[3,3,256,256]{3,2,1,0:T(8,128)})) %all-reduce.7.cloned.1.call-update) | async-done | bytes 3473424 | tf_op jit(solution)/shard_map/psum | solution.py:129
  227.8 0.9 fusion.4
  229.0 0.9 all_to_all.23
  229.9 217.0 %all-reduce.5.cloned.1.call-done = (f32[3,3,128,128]{3,2,1,0:T(8,128)}, f32[2,2,128,256]{3,2,1,0:T(8,128)}, f32[3,3,256,256]{3,2,1,0:T(8,128)}) async-done(((f32[3,3,128,128]{3,2,1,0:T(8,128)}, f32[2,2,128,256]{3,2,1,0:T(8,128)}, f32[3,3,256,256]{3,2,1,0:T(8,128)}), (f32[3,3,128,128]{3,2,1,0:T(8,128)}, f32[2,2,128,256]{3,2,1,0:T(8,128)}, f32[3,3,256,256]{3,2,1,0:T(8,128)})) %all-reduce.5.cloned.1.call-update) | async-done | bytes 3473424 | tf_op jit(solution)/shard_map/psum | solution.py:129
  446.9 1.9 multiply_convert_fusion.1
  448.8 0.7 multiply_convert_fusion.2
  449.5 2.9 multiply_convert_fusion
  (177 shorter events, 11.9 us)
Async XLA Ops:
  7.2 30.4 %copy-start = (bf16[2,2,128,256]{3,2,1,0:T(8,128)(2,1)S(1)}, bf16[2,2,128,256]{3,2,1,0:T(8,128)(2,1)}, u32[]{:S(2)}) copy-start(bf16[2,2,128,256]{3,2,1,0:T(8,128)(2,1)} %param.7) | copy-start | bytes 786436
  7.2 20.3 %copy-start.2 = (bf16[8,64,128]{2,1,0:T(8,128)(2,1)S(1)}, bf16[8,64,128]{2,1,0:T(8,128)(2,1)}, u32[]{:S(2)}) copy-start(bf16[8,64,128]{2,1,0:T(8,128)(2,1)} %param.5) | copy-start | bytes 393220
  7.2 25.0 %copy-start.15 = (bf16[3,3,128,128]{3,2,1,0:T(8,128)(2,1)S(1)}, bf16[3,3,128,128]{3,2,1,0:T(8,128)(2,1)}, u32[]{:S(2)}) copy-start(bf16[3,3,128,128]{3,2,1,0:T(8,128)(2,1)} %param.6) | copy-start | bytes 884740
  8.0 16.0 %collective-permute-start = (bf16[1,64,128]{2,1,0:T(8,128)(2,1)S(1)}, bf16[1,64,128]{2,1,0:T(8,128)(2,1)S(1)}, u32[]{:S(2)}, u32[]{:S(2)}) collective-permute-start(bf16[1,64,128]{2,1,0:T(8,128)(2,1)S(1)} %get-tuple-element.42), channel_id=1, source_target_pairs={{0,16},{16,32},{32,48},{48,64},{64,80},{80,96},{96,112},{112,128},... | collective-permute-start | bytes 49160 | tf_op jit(solution)/shard_map/ppermute | solution.py:16
  15.3 39.1 %all-to-all-start.1 = ((bf16[16,2,1024]{2,1,0:T(2,128)(2,1)}), bf16[16,2,1024]{2,1,0:T(2,128)(2,1)S(1)}, u32[]{:S(2)}, u32[]{:S(2)}) async-start(bf16[16,2,1024]{2,1,0:T(2,128)(2,1)} %reshape.213), calls=%async_computation.1 | async-start | bytes 131072 | tf_op jit(solution)/shard_map/all_to_all | solution.py:91
  22.1 204.4 %all-reduce.7.cloned.1.call-start = ((), (), s32[]{:S(2)}) async-start(), calls=%async_computation.3 | async-start | bytes 6946816 | tf_op jit(solution)/shard_map/psum | solution.py:129
  22.1 5.4 %collective-permute-start.1 = (bf16[1,64,128]{2,1,0:T(8,128)(2,1)S(1)}, bf16[1,64,128]{2,1,0:T(8,128)(2,1)S(1)}, u32[]{:S(2)}, u32[]{:S(2)}) collective-permute-start(bf16[1,64,128]{2,1,0:T(8,128)(2,1)S(1)} %get-tuple-element.41), channel_id=1, source_target_pairs={{16,0},{32,16},{48,32},{64,48},{80,64},{96,80},{112,96},{128,112},... | collective-permute-start | bytes 49160 | tf_op jit(solution)/shard_map/ppermute | solution.py:18
  27.5 4.6 %copy-start.3 = (bf16[8,64,128]{2,1,0:T(8,128)(2,1)}, bf16[8,64,128]{2,1,0:T(8,128)(2,1)S(1)}, u32[]{:S(2)}) copy-start(bf16[8,64,128]{2,1,0:T(8,128)(2,1)S(1)} %get-tuple-element.40) | copy-start | bytes 393220
  27.6 4.9 %collective-permute-start.2 = (bf16[10,1,128]{2,1,0:T(2,128)(2,1)S(1)}, bf16[10,1,128]{2,1,0:T(2,128)(2,1)S(1)}, u32[]{:S(2)}, u32[]{:S(2)}) collective-permute-start(bf16[10,1,128]{2,1,0:T(2,128)(2,1)S(1)} %get-tuple-element.30), channel_id=1, source_target_pairs={{0,1},{1,2},{2,3},{3,4},{4,5},{5,6},{6,7},{7,8},{8,9},{9,10},{10,1... | collective-permute-start | bytes 7688 | tf_op jit(solution)/shard_map/ppermute | solution.py:16
  30.9 4.4 collective-permute-start.3
  36.6 6.8 %copy-start.1 = (bf16[3,3,256,256]{3,2,1,0:T(8,128)(2,1)S(1)}, bf16[3,3,256,256]{3,2,1,0:T(8,128)(2,1)}, u32[]{:S(2)}) copy-start(bf16[3,3,256,256]{3,2,1,0:T(8,128)(2,1)} %param.8) | copy-start | bytes 3538948
  37.6 2.1 copy-start.32
  37.8 5.7 %collective-permute-start.5 = (bf16[1,32,256]{2,1,0:T(8,128)(2,1)S(1)}, bf16[1,32,256]{2,1,0:T(8,128)(2,1)S(1)}, u32[]{:S(2)}, u32[]{:S(2)}) collective-permute-start(bf16[1,32,256]{2,1,0:T(8,128)(2,1)S(1)} %get-tuple-element.70), channel_id=1, source_target_pairs={{16,0},{32,16},{48,32},{64,48},{80,64},{96,80},{112,96},{128,112},... | collective-permute-start | bytes 49160 | tf_op jit(solution)/shard_map/ppermute | solution.py:18
  39.7 4.5 collective-permute-start.4
  44.2 5.2 %collective-permute-start.6 = (bf16[6,1,256]{2,1,0:T(2,128)(2,1)S(1)}, bf16[6,1,256]{2,1,0:T(2,128)(2,1)S(1)}, u32[]{:S(2)}, u32[]{:S(2)}) collective-permute-start(bf16[6,1,256]{2,1,0:T(2,128)(2,1)S(1)} %get-tuple-element.61), channel_id=1, source_target_pairs={{0,1},{1,2},{2,3},{3,4},{4,5},{5,6},{6,7},{7,8},{8,9},{9,10},{10,1... | collective-permute-start | bytes 9224 | tf_op jit(solution)/shard_map/ppermute | solution.py:16
  47.3 4.4 collective-permute-start.7
  51.8 1.7 copy-start.17
  51.8 1.7 copy-start.19
  51.8 1.7 copy-start.21
  51.8 1.7 copy-start.23
  51.8 1.7 copy-start.25
  51.8 1.7 copy-start.27
  57.9 2.4 copy-start.28
  57.9 2.6 copy-start.37
  57.9 2.8 copy-start.26
  58.9 2.3 copy-start.29
  58.9 2.0 copy-start.24
  60.2 1.2 copy-start.22
  60.3 1.3 copy-start.20
  60.7 1.3 copy-start.18
  62.3 9.3 %collective-permute-start.9 = (bf16[1,32,256]{2,1,0:T(8,128)(2,1)S(1)}, bf16[1,32,256]{2,1,0:T(8,128)(2,1)S(1)}, u32[]{:S(2)}, u32[]{:S(2)}) collective-permute-start(bf16[1,32,256]{2,1,0:T(8,128)(2,1)S(1)} %get-tuple-element.66), channel_id=1, source_target_pairs={{16,0},{32,16},{48,32},{64,48},{80,64},{96,80},{112,96},{128,112},... | collective-permute-start | bytes 49160 | tf_op jit(solution)/shard_map/ppermute | solution.py:18
  64.4 7.2 %collective-permute-start.8 = (bf16[1,32,256]{2,1,0:T(8,128)(2,1)S(1)}, bf16[1,32,256]{2,1,0:T(8,128)(2,1)S(1)}, u32[]{:S(2)}, u32[]{:S(2)}) collective-permute-start(bf16[1,32,256]{2,1,0:T(8,128)(2,1)S(1)} %get-tuple-element.65), channel_id=1, source_target_pairs={{0,16},{16,32},{32,48},{48,64},{64,80},{80,96},{96,112},{112,128},... | collective-permute-start | bytes 49160 | tf_op jit(solution)/shard_map/ppermute | solution.py:16
  71.6 5.9 %collective-permute-start.10 = (bf16[6,1,256]{2,1,0:T(2,128)(2,1)S(1)}, bf16[6,1,256]{2,1,0:T(2,128)(2,1)S(1)}, u32[]{:S(2)}, u32[]{:S(2)}) collective-permute-start(bf16[6,1,256]{2,1,0:T(2,128)(2,1)S(1)} %get-tuple-element.57), channel_id=1, source_target_pairs={{0,1},{1,2},{2,3},{3,4},{4,5},{5,6},{6,7},{7,8},{8,9},{9,10},{10,1... | collective-permute-start | bytes 9224 | tf_op jit(solution)/shard_map/ppermute | solution.py:16
  76.0 4.7 %collective-permute-start.11 = (bf16[6,1,256]{2,1,0:T(2,128)(2,1)S(1)}, bf16[6,1,256]{2,1,0:T(2,128)(2,1)S(1)}, u32[]{:S(2)}, u32[]{:S(2)}) collective-permute-start(bf16[6,1,256]{2,1,0:T(2,128)(2,1)S(1)} %get-tuple-element.58), channel_id=1, source_target_pairs={{1,0},{2,1},{3,2},{4,3},{5,4},{6,5},{7,6},{8,7},{9,8},{10,9},{11,1... | collective-permute-start | bytes 9224 | tf_op jit(solution)/shard_map/ppermute | solution.py:18
  82.4 1.2 copy-start.35
  82.7 1.2 copy-start.14
  82.9 1.4 copy-start.12
  82.9 1.6 copy-start.10
  83.3 1.7 copy-start.8
  83.6 1.7 copy-start.33
  87.3 6.6 %copy-start.16 = (bf16[3,3,128,128]{3,2,1,0:T(8,128)(2,1)S(1)}, bf16[3,3,128,128]{3,2,1,0:T(8,128)(2,1)}, u32[]{:S(2)}) copy-start(bf16[3,3,128,128]{3,2,1,0:T(8,128)(2,1)} %param.6) | copy-start | bytes 884740
  87.3 15.8 %collective-permute-start.13 = (bf16[1,64,128]{2,1,0:T(8,128)(2,1)S(1)}, bf16[1,64,128]{2,1,0:T(8,128)(2,1)S(1)}, u32[]{:S(2)}, u32[]{:S(2)}) collective-permute-start(bf16[1,64,128]{2,1,0:T(8,128)(2,1)S(1)} %get-tuple-element.35), channel_id=1, source_target_pairs={{16,0},{32,16},{48,32},{64,48},{80,64},{96,80},{112,96},{128,112},... | collective-permute-start | bytes 49160 | tf_op jit(solution)/shard_map/ppermute | solution.py:18
  89.4 13.8 %collective-permute-start.12 = (bf16[1,64,128]{2,1,0:T(8,128)(2,1)S(1)}, bf16[1,64,128]{2,1,0:T(8,128)(2,1)S(1)}, u32[]{:S(2)}, u32[]{:S(2)}) collective-permute-start(bf16[1,64,128]{2,1,0:T(8,128)(2,1)S(1)} %get-tuple-element.34), channel_id=1, source_target_pairs={{0,16},{16,32},{32,48},{48,64},{64,80},{80,96},{96,112},{112,128},... | collective-permute-start | bytes 49160 | tf_op jit(solution)/shard_map/ppermute | solution.py:16
  95.0 133.7 %all-to-all-start = ((bf16[16,2,1024]{2,1,0:T(2,128)(2,1)}), bf16[16,2,1024]{2,1,0:T(2,128)(2,1)S(1)}, u32[]{:S(2)}, u32[]{:S(2)}) async-start(bf16[16,2,1024]{2,1,0:T(2,128)(2,1)} %reshape.211), calls=%async_computation | async-start | bytes 131072 | tf_op jit(solution)/shard_map/all_to_all | solution.py:90
  103.1 343.8 %all-reduce.5.cloned.1.call-start = ((), (), s32[]{:S(2)}) async-start(), calls=%async_computation.2 | async-start | bytes 6946816 | tf_op jit(solution)/shard_map/psum | solution.py:129
  103.1 4.8 %collective-permute-start.14 = (bf16[10,1,128]{2,1,0:T(2,128)(2,1)S(1)}, bf16[10,1,128]{2,1,0:T(2,128)(2,1)S(1)}, u32[]{:S(2)}, u32[]{:S(2)}) collective-permute-start(bf16[10,1,128]{2,1,0:T(2,128)(2,1)S(1)} %get-tuple-element.25), channel_id=1, source_target_pairs={{0,1},{1,2},{2,3},{3,4},{4,5},{5,6},{6,7},{7,8},{8,9},{9,10},{10,1... | collective-permute-start | bytes 7688 | tf_op jit(solution)/shard_map/ppermute | solution.py:16
  106.4 4.4 collective-permute-start.15
  446.9 1.9 copy-start.31
  (10 other events, 9.0 us)
Sparse Core Ops, SparseCore 0:
  87.4 138.9 all-reduce.6
  229.2 217.6 all-reduce.4
